TPU v7x, 256 devices: a whole 4x4x8 slice. The times are simulated.
256 devices in a mesh: sx: 8 (over z), sy: 32 (over y, x, core).
Axes of the slice: x: 4, y: 4, z: 8, core: 2. Of those that a mesh axis runs over, the one named last changes fastest.
Arguments:
- loads: float32 [12288, 4096], P('sx', 'sy'), may hold values from -6 to 6
- dual_op: bfloat16 [12288, 49152], P('sx', 'sy'), as said below
- dirichlet: bfloat16 [12288, 49152], P('sx', 'sy'), as said below
- corner_coupling: bfloat16 [128, 49152], P('sx', 'sy'), may hold values from -0.625 to 0.625
- corner_map: int32 [8, 512], P('sx', 'sy'), may hold values from 0 to 2047, as said below
- coarse_inverse: float32 [2048, 2048], P('sy'), as said below
Outputs:
- multipliers: float32 [12288, 4096], P('sx', 'sy')
- residual: float32 [12288, 4096], P('sx', 'sy')
Inputs may be any that keep to these rules, and one draw needn't show every extreme that they name: `corner_map`: every coarse unknown is named by exactly two entries over all subdomains. `dual_op`: each subdomain's block is symmetric positive definite. `dirichlet`: each subdomain's block is symmetric positive definite. `coarse_inverse`: symmetric positive definite.
All inputs are finite; a program needn't handle non-finite values.
Results may differ from a plain program's by a relative error of at most 0.014.
Values sent between devices are 32-bit elements; how exact they have to be, the bound alone decides.
No kernel may reach another device: no remote copies, remote signals or barrier semaphores. Data moves between devices by JAX's collectives and lax.ppermute only.
A program may use at most 64 MiB of HBM per device.

v0:
```python
import jax
import jax.numpy as jnp
from jax import lax
from jax.sharding import PartitionSpec as P

FACE = 320
EDGE = 64
ITERS = 4
HALF = 0.5
HIGH = lax.Precision.HIGHEST


def passed_along(value, axis, steps):
    count = lax.axis_size(axis)
    first, last = (max(0, -steps), min(count, count - steps))
    return lax.ppermute(value, axis, [(source, source + steps) for source in range(first, last)])


def padded(block, sides, width):
    for axis, dim in sides:
        count = lax.axis_size(axis)
        forward = [(i, i + 1) for i in range(count - 1)]
        backward = [(target, source) for source, target in forward]
        low = lax.ppermute(
            lax.slice_in_dim(block, block.shape[dim] - width, None, axis=dim), axis, forward
        )
        high = lax.ppermute(lax.slice_in_dim(block, 0, width, axis=dim), axis, backward)
        block = jnp.concatenate([low, block, high], axis=dim)
    return block


def split_blocks(field):
    widths = [FACE, FACE, FACE, FACE, EDGE, EDGE, EDGE, EDGE]
    pieces = []
    start = 0
    for width in widths:
        pieces.append(field[start : start + width])
        start = start + width
    return pieces


def assemble(field):
    pieces = split_blocks(field)
    upper_face = passed_along(pieces[1], "sx", 1)
    lower_face = passed_along(pieces[0], "sx", -1)
    left_face = passed_along(pieces[3], "sy", 1)
    right_face = passed_along(pieces[2], "sy", -1)
    stacked = jnp.concatenate([pieces[4], pieces[5], pieces[6], pieces[7]], axis=0)[None, None]
    bordered = padded(stacked, (("sx", 0), ("sy", 1)), 1)
    incoming = [
        upper_face,
        lower_face,
        left_face,
        right_face,
        bordered[0, 0, 3 * EDGE : 4 * EDGE],
        bordered[0, 2, 2 * EDGE : 3 * EDGE],
        bordered[2, 0, EDGE : 2 * EDGE],
        bordered[2, 2, 0:EDGE],
    ]
    return jnp.concatenate([mine + HALF * theirs for mine, theirs in zip(pieces, incoming)], axis=0)


def operate(direction, dual_op, corner_coupling, selector, coarse_inverse):
    spread = assemble(direction)
    rounded = spread.astype(jnp.bfloat16)
    local = jnp.dot(dual_op, rounded, preferred_element_type=jnp.float32)
    corner_part = jnp.dot(corner_coupling, rounded, preferred_element_type=jnp.float32)
    scattered = jnp.dot(selector.T, corner_part, precision=HIGH)
    coarse_sum = lax.psum(scattered, ("sx", "sy"))
    owned_rows = jnp.dot(coarse_inverse, coarse_sum, precision=HIGH)
    solution = lax.all_gather(owned_rows, "sy", axis=0, tiled=True)
    picked = jnp.dot(selector, solution, precision=HIGH)
    correction = jnp.dot(corner_coupling.astype(jnp.float32).T, picked, precision=HIGH)
    return assemble(local + correction)


def residual_norm(residual, smoothed):
    return lax.psum(jnp.sum(residual * smoothed, axis=0), ("sx", "sy"))


def body(loads, dual_op, dirichlet, corner_coupling, corner_map, coarse_inverse):
    corners = corner_map.shape[1]
    coarse_order = coarse_inverse.shape[1]
    selector = (
        corner_map[0][:, None] == lax.broadcasted_iota(jnp.int32, (corners, coarse_order), 1)
    ).astype(jnp.float32)

    def smooth(residual):
        return jnp.dot(dirichlet, residual.astype(jnp.bfloat16), preferred_element_type=jnp.float32)

    multipliers = jnp.zeros_like(loads)
    residual = loads
    smoothed = smooth(residual)
    direction = smoothed
    current = residual_norm(residual, smoothed)
    for step in range(ITERS):
        image = operate(direction, dual_op, corner_coupling, selector, coarse_inverse)
        alpha = current / lax.psum(jnp.sum(direction * image, axis=0), ("sx", "sy"))
        multipliers = multipliers + alpha * direction
        residual = residual - alpha * image
        if step + 1 < ITERS:
            smoothed = smooth(residual)
            following = residual_norm(residual, smoothed)
            direction = smoothed + following / current * direction
            current = following
    return (multipliers, residual)


def solution(mesh):
    in_specs = (
        P("sx", "sy"),
        P("sx", "sy"),
        P("sx", "sy"),
        P("sx", "sy"),
        P("sx", "sy"),
        P("sy", None),
    )
    out_specs = (P("sx", "sy"), P("sx", "sy"))
    return jax.shard_map(body, mesh=mesh, in_specs=in_specs, out_specs=out_specs, check_vma=False)
```

profile of v0, /device:TPU:1, one launch (start us, length us, event | category | flops | bytes accessed | tf_op | source)
XLA Modules:
  0.0 2106.7 jit_solution(1776008902199709787)
XLA Ops:
  12.6 5.0 collective-permute-start.4
  37.2 4.4 collective-permute-done.7
  43.7 265.5 %all-reduce.6.cloned.1.call-done = f32[2048,128]{1,0:T(8,128)} async-done(((f32[2048,128]{1,0:T(8,128)}), f32[2048,128]{1,0:T(8,128)}) %all-reduce.6.cloned.1.call-update) | async-done | bytes 1048592 | tf_op jit(solution)/shard_map/psum | solution.py:69
  315.6 45.0 %all-gather.5.cloned.1.call-done = f32[2048,128]{1,0:T(8,128)} async-done(((f32[64,128]{1,0:T(8,128)}), f32[2048,128]{1,0:T(8,128)}) %all-gather.5.cloned.1.call-update) | async-done | bytes 1048592 | tf_op jit(solution)/shard_map/all_gather | solution.py:71
  373.4 4.5 collective-permute-start.14
  385.7 4.4 collective-permute-done.11
  391.3 82.7 %all-reduce = (f32[128]{0:T(128)S(1)}, f32[128]{0:T(128)S(1)}) all-reduce(f32[128]{0:T(128)S(1)} %get-tuple-element.3, f32[128]{0:T(128)S(1)} %get-tuple-element.2), channel_id=1, replica_groups=mesh['sx'=8,'sy'=32] {'sx','sy'}, use_global_device_ids=true, to_apply=%region_1.0 | all-reduce | flops 256 | bytes 2048 | tf_op jit(solution)/shard_map/psum | solution.py:78
  475.3 4.6 multiply_reduce_fusion.5
  479.9 74.7 %psum.87 = f32[128]{0:T(128)S(1)} all-reduce(f32[128]{0:T(128)S(1)} %get-tuple-element.40), channel_id=1, replica_groups=mesh['sx'=8,'sy'=32] {'sx','sy'}, use_global_device_ids=true, to_apply=%region_6.0 | all-reduce | flops 128 | bytes 1024 | tf_op jit(solution)/shard_map/psum | solution.py:78
  578.8 4.4 collective-permute-done.23
  585.6 263.1 %all-reduce.8.cloned.1.call-done = f32[2048,128]{1,0:T(8,128)} async-done(((f32[2048,128]{1,0:T(8,128)}), f32[2048,128]{1,0:T(8,128)}) %all-reduce.8.cloned.1.call-update) | async-done | bytes 1048592 | tf_op jit(solution)/shard_map/psum | solution.py:69
  851.3 4.6 fusion.123
  856.0 44.0 %all-gather.7.cloned.1.call-done = f32[2048,128]{1,0:T(8,128)} async-done(((f32[64,128]{1,0:T(8,128)}), f32[2048,128]{1,0:T(8,128)}) %all-gather.7.cloned.1.call-update) | async-done | bytes 1048592 | tf_op jit(solution)/shard_map/all_gather | solution.py:71
  913.8 4.5 collective-permute-start.30
  931.7 82.7 %psum.89 = f32[128]{0:T(128)S(1)} all-reduce(f32[128]{0:T(128)S(1)} %multiply_reduce_fusion.4), channel_id=1, replica_groups=mesh['sx'=8,'sy'=32] {'sx','sy'}, use_global_device_ids=true, to_apply=%region_9.0 | all-reduce | flops 128 | bytes 1024 | tf_op jit(solution)/shard_map/psum | solution.py:98
  1016.5 4.6 multiply_reduce_fusion.3
  1021.2 74.7 %psum.90 = f32[128]{0:T(128)S(1)} all-reduce(f32[128]{0:T(128)S(1)} %get-tuple-element.42), channel_id=1, replica_groups=mesh['sx'=8,'sy'=32] {'sx','sy'}, use_global_device_ids=true, to_apply=%region_11.0 | all-reduce | flops 128 | bytes 1024 | tf_op jit(solution)/shard_map/psum | solution.py:78
  1120.1 4.4 collective-permute-done.39
  1126.6 263.3 %all-reduce.10.cloned.1.call-done = f32[2048,128]{1,0:T(8,128)} async-done(((f32[2048,128]{1,0:T(8,128)}), f32[2048,128]{1,0:T(8,128)}) %all-reduce.10.cloned.1.call-update) | async-done | bytes 1048592 | tf_op jit(solution)/shard_map/psum | solution.py:69
  1392.6 4.6 fusion.124
  1397.2 43.7 %all-gather.9.cloned.1.call-done = f32[2048,128]{1,0:T(8,128)} async-done(((f32[64,128]{1,0:T(8,128)}), f32[2048,128]{1,0:T(8,128)}) %all-gather.9.cloned.1.call-update) | async-done | bytes 1048592 | tf_op jit(solution)/shard_map/all_gather | solution.py:71
  1454.8 4.5 collective-permute-start.46
  1472.7 82.7 %psum.92 = f32[128]{0:T(128)S(1)} all-reduce(f32[128]{0:T(128)S(1)} %multiply_reduce_fusion.2), channel_id=1, replica_groups=mesh['sx'=8,'sy'=32] {'sx','sy'}, use_global_device_ids=true, to_apply=%region_14.0 | all-reduce | flops 128 | bytes 1024 | tf_op jit(solution)/shard_map/psum | solution.py:98
  1557.8 4.6 multiply_reduce_fusion.1
  1562.4 74.8 %psum.93 = f32[128]{0:T(128)S(1)} all-reduce(f32[128]{0:T(128)S(1)} %get-tuple-element.44), channel_id=1, replica_groups=mesh['sx'=8,'sy'=32] {'sx','sy'}, use_global_device_ids=true, to_apply=%region_16.0 | all-reduce | flops 128 | bytes 1024 | tf_op jit(solution)/shard_map/psum | solution.py:78
  1661.4 4.4 collective-permute-done.55
  1667.9 263.3 %all-reduce.12.cloned.1.call-done = f32[2048,128]{1,0:T(8,128)} async-done(((f32[2048,128]{1,0:T(8,128)}), f32[2048,128]{1,0:T(8,128)}) %all-reduce.12.cloned.1.call-update) | async-done | bytes 1048592 | tf_op jit(solution)/shard_map/psum | solution.py:69
  1933.9 4.6 fusion.125
  1938.5 43.8 %all-gather.11.cloned.1.call-done = f32[2048,128]{1,0:T(8,128)} async-done(((f32[64,128]{1,0:T(8,128)}), f32[2048,128]{1,0:T(8,128)}) %all-gather.11.cloned.1.call-update) | async-done | bytes 1048592 | tf_op jit(solution)/shard_map/all_gather | solution.py:71
  1996.2 4.5 collective-permute-start.62
  2008.5 4.4 collective-permute-done.59
  2014.1 82.7 %psum.95 = f32[128]{0:T(128)S(1)} all-reduce(f32[128]{0:T(128)S(1)} %multiply_reduce_fusion), channel_id=1, replica_groups=mesh['sx'=8,'sy'=32] {'sx','sy'}, use_global_device_ids=true, to_apply=%region_19.0 | all-reduce | flops 128 | bytes 1024 | tf_op jit(solution)/shard_map/psum | solution.py:98
  (285 shorter events, 227.6 us)
Async XLA Ops:
  7.2 302.0 %all-reduce.6.cloned.1.call-start = ((), (), s32[]{:S(2)}) async-start(), calls=%async_computation | async-start | bytes 2097152 | tf_op jit(solution)/shard_map/psum | solution.py:69
  11.3 15.6 collective-permute-start.5
  12.6 16.2 collective-permute-start.4
  17.6 14.8 collective-permute-start
  21.2 13.3 collective-permute-start.1
  43.7 316.9 %all-gather.5.cloned.1.call-start = ((), (), s32[]{:S(2)}) async-start(), calls=%async_computation.1 | async-start | bytes 1081344 | tf_op jit(solution)/shard_map/all_gather | solution.py:71
  311.8 536.8 %all-reduce.8.cloned.1.call-start = ((), (), s32[]{:S(2)}) async-start(), calls=%async_computation.2 | async-start | bytes 2097152 | tf_op jit(solution)/shard_map/psum | solution.py:69
  371.5 13.9 collective-permute-start.9
  373.4 16.7 collective-permute-start.14
  555.8 12.7 collective-permute-start.21
  557.1 13.3 collective-permute-start.20
  561.2 13.0 collective-permute-start.16
  563.1 13.0 collective-permute-start.17
  585.3 314.6 %all-gather.7.cloned.1.call-start = ((), (), s32[]{:S(2)}) async-start(), calls=%async_computation.3 | async-start | bytes 1081344 | tf_op jit(solution)/shard_map/all_gather | solution.py:71
  851.3 538.6 %all-reduce.10.cloned.1.call-start = ((), (), s32[]{:S(2)}) async-start(), calls=%async_computation.4 | async-start | bytes 2097152 | tf_op jit(solution)/shard_map/psum | solution.py:69
  911.9 13.9 collective-permute-start.25
  913.8 16.7 collective-permute-start.30
  1097.1 12.7 collective-permute-start.37
  1098.4 13.3 collective-permute-start.36
  1102.4 13.0 collective-permute-start.32
  1104.4 13.0 collective-permute-start.33
  1126.6 314.4 %all-gather.9.cloned.1.call-start = ((), (), s32[]{:S(2)}) async-start(), calls=%async_computation.5 | async-start | bytes 1081344 | tf_op jit(solution)/shard_map/all_gather | solution.py:71
  1392.6 538.7 %all-reduce.12.cloned.1.call-start = ((), (), s32[]{:S(2)}) async-start(), calls=%async_computation.6 | async-start | bytes 2097152 | tf_op jit(solution)/shard_map/psum | solution.py:69
  1452.9 14.1 collective-permute-start.41
  1454.8 16.7 collective-permute-start.46
  1638.5 12.5 collective-permute-start.53
  1639.8 13.2 collective-permute-start.52
  1643.8 12.8 collective-permute-start.48
  1645.8 12.9 collective-permute-start.49
  1667.9 314.4 %all-gather.11.cloned.1.call-start = ((), (), s32[]{:S(2)}) async-start(), calls=%async_computation.7 | async-start | bytes 1081344 | tf_op jit(solution)/shard_map/all_gather | solution.py:71
  1994.3 13.9 collective-permute-start.57
  1996.2 16.7 collective-permute-start.62
  (52 other events, 842.2 us)
Sparse Core Ops, SparseCore 0:
  43.8 265.3 all-reduce.5
  312.3 48.2 all-gather.4
  585.4 263.1 all-reduce.7
  851.6 48.2 all-gather.6
  1126.7 263.1 all-reduce.9
  1392.7 48.2 all-gather.8
  1668.0 263.2 all-reduce.11
  1934.0 48.2 all-gather.10
where the time goes:
time: 2110 us
  waiting for transfers between devices  1280 us (61%)
  blocking collectives  555 us (26%)
  starting transfers between devices  171 us (8%)
  matrix products  66.4 us (3%)
    psum x4, waiting for transfers between devices, operate(): coarse_sum = lax.psum(scattered, ('sx', 'sy'))  1060 us
    psum x4, blocking collectives, residual_norm(): return lax.psum(jnp.sum(residual * smoothed, axis=0), ('sx', 'sy'))  307 us
    psum x3, blocking collectives, body(): alpha = current / lax.psum(jnp.sum(direction * image, axis=0), ('sx', 'sy'))  248 us
    all_gather x4, waiting for transfers between devices, operate(): solution = lax.all_gather(owned_rows, 'sy', axis=0, tiled=True)  176 us
    ppermute x32, starting transfers between devices, passed_along(): lax.ppermute(value, axis, [(source, source + steps) for source in range(f...  79 us
    ppermute x16, starting transfers between devices, padded(): lax.ppermute(lax.slice_in_dim(block, block.shape[dim] - width, None, axis...  65.3 us
  transfers between devices with their start and end apart: 72, of which 28 were waited for; matrix products, arithmetic and copies ran while one was open for 1% of the time, Pallas kernels for 0%

commit v1 on v0

--- a/solution.py
+++ b/solution.py
@@ -95,7 +95,7 @@
     current = residual_norm(residual, smoothed)
     for step in range(ITERS):
         image = operate(direction, dual_op, corner_coupling, selector, coarse_inverse)
-        alpha = current / lax.psum(jnp.sum(direction * image, axis=0), ("sx", "sy"))
+        alpha = current / lax.psum(lax.psum(jnp.sum(direction * image, axis=0), "sx"), "sy")
         multipliers = multipliers + alpha * direction
         residual = residual - alpha * image
         if step + 1 < ITERS:

time: 2110 us -> 2170 us (1.028)
  blocking collectives: 555 us -> 617 us
    psum x3 -> x8, blocking collectives: 248 us -> 313 us  [the longest x4 254 us: body(): lax.psum(lax.psum(jnp.sum(direction * image, axis=0), 'sx'), 'sy')]
where the time goes in v1:
time: 2170 us; the launch traced here: 2160 us
  waiting for transfers between devices  1280 us (59%)
  blocking collectives  617 us (28%)
  starting transfers between devices  170 us (8%)
  matrix products  66.4 us (3%)
    psum x4, waiting for transfers between devices, operate(): coarse_sum = lax.psum(scattered, ('sx', 'sy'))  1050 us
    psum x4, blocking collectives, residual_norm(): return lax.psum(jnp.sum(residual * smoothed, axis=0), ('sx', 'sy'))  304 us
    psum x4, blocking collectives, body(): lax.psum(lax.psum(jnp.sum(direction * image, axis=0), 'sx'), 'sy')  254 us
    all_gather x4, waiting for transfers between devices, operate(): solution = lax.all_gather(owned_rows, 'sy', axis=0, tiled=True)  176 us
    ppermute x32, starting transfers between devices, passed_along(): lax.ppermute(value, axis, [(source, source + steps) for source in range(f...  77.7 us
    ppermute x16, starting transfers between devices, padded(): lax.ppermute(lax.slice_in_dim(block, block.shape[dim] - width, None, axis...  65.6 us
    psum x4, blocking collectives, body(): lax.psum(jnp.sum(direction * image, axis=0), 'sx')  58.6 us
  transfers between devices with their start and end apart: 72, of which 28 were waited for; matrix products, arithmetic and copies ran while one was open for 1% of the time, Pallas kernels for 0%

profile of v1, /device:TPU:1, one launch (start us, length us, event | category | flops | bytes accessed | tf_op | source)
XLA Modules:
  0.0 2164.9 jit_solution(225033356254219687)
XLA Ops:
  12.6 5.0 collective-permute-start.4
  37.2 4.4 collective-permute-done.7
  43.7 265.5 %all-reduce.5.cloned.1.call-done = f32[2048,128]{1,0:T(8,128)} async-done(((f32[2048,128]{1,0:T(8,128)}), f32[2048,128]{1,0:T(8,128)}) %all-reduce.5.cloned.1.call-update) | async-done | bytes 1048592 | tf_op jit(solution)/shard_map/psum | solution.py:69
  315.6 45.0 %all-gather.5.cloned.1.call-done = f32[2048,128]{1,0:T(8,128)} async-done(((f32[64,128]{1,0:T(8,128)}), f32[2048,128]{1,0:T(8,128)}) %all-gather.5.cloned.1.call-update) | async-done | bytes 1048592 | tf_op jit(solution)/shard_map/all_gather | solution.py:71
  373.4 4.5 collective-permute-start.14
  391.3 82.7 %psum.112 = f32[128]{0:T(128)S(1)} all-reduce(f32[128]{0:T(128)S(1)} %get-tuple-element.3), channel_id=1, replica_groups=mesh['sx'=8,'sy'=32] {'sx','sy'}, use_global_device_ids=true, to_apply=%region_1.0 | all-reduce | flops 128 | bytes 1024 | tf_op jit(solution)/shard_map/psum | solution.py:78
  474.1 13.6 psum.114
  487.7 66.4 %psum.115 = f32[128]{0:T(128)S(1)} all-reduce(f32[128]{0:T(128)S(1)} %psum.114), channel_id=1, replica_groups=mesh['sx'=8,'sy'=32] {'sy'}, use_global_device_ids=true, to_apply=%region_5.0 | all-reduce | flops 128 | bytes 1024 | tf_op jit(solution)/shard_map/psum | solution.py:98
  555.4 4.6 multiply_reduce_fusion.5
  560.0 72.6 %psum.116 = f32[128]{0:T(128)S(1)} all-reduce(f32[128]{0:T(128)S(1)} %get-tuple-element.38), channel_id=1, replica_groups=mesh['sx'=8,'sy'=32] {'sx','sy'}, use_global_device_ids=true, to_apply=%region_7.0 | all-reduce | flops 128 | bytes 1024 | tf_op jit(solution)/shard_map/psum | solution.py:78
  664.1 261.5 %all-reduce.7.cloned.1.call-done = f32[2048,128]{1,0:T(8,128)} async-done(((f32[2048,128]{1,0:T(8,128)}), f32[2048,128]{1,0:T(8,128)}) %all-reduce.7.cloned.1.call-update) | async-done | bytes 1048592 | tf_op jit(solution)/shard_map/psum | solution.py:69
  928.3 4.6 fusion.123
  932.9 44.0 %all-gather.7.cloned.1.call-done = f32[2048,128]{1,0:T(8,128)} async-done(((f32[64,128]{1,0:T(8,128)}), f32[2048,128]{1,0:T(8,128)}) %all-gather.7.cloned.1.call-update) | async-done | bytes 1048592 | tf_op jit(solution)/shard_map/all_gather | solution.py:71
  990.8 4.5 collective-permute-start.30
  1008.6 15.0 psum.118
  1023.6 62.5 %psum.119 = f32[128]{0:T(128)S(1)} all-reduce(f32[128]{0:T(128)S(1)} %psum.118), channel_id=1, replica_groups=mesh['sx'=8,'sy'=32] {'sy'}, use_global_device_ids=true, to_apply=%region_11.0 | all-reduce | flops 128 | bytes 1024 | tf_op jit(solution)/shard_map/psum | solution.py:98
  1088.3 4.6 multiply_reduce_fusion.3
  1092.9 74.3 %psum.120 = f32[128]{0:T(128)S(1)} all-reduce(f32[128]{0:T(128)S(1)} %get-tuple-element.40), channel_id=1, replica_groups=mesh['sx'=8,'sy'=32] {'sx','sy'}, use_global_device_ids=true, to_apply=%region_13.0 | all-reduce | flops 128 | bytes 1024 | tf_op jit(solution)/shard_map/psum | solution.py:78
  1197.1 263.0 %all-reduce.9.cloned.1.call-done = f32[2048,128]{1,0:T(8,128)} async-done(((f32[2048,128]{1,0:T(8,128)}), f32[2048,128]{1,0:T(8,128)}) %all-reduce.9.cloned.1.call-update) | async-done | bytes 1048592 | tf_op jit(solution)/shard_map/psum | solution.py:69
  1462.8 4.6 fusion.124
  1467.4 43.7 %all-gather.9.cloned.1.call-done = f32[2048,128]{1,0:T(8,128)} async-done(((f32[64,128]{1,0:T(8,128)}), f32[2048,128]{1,0:T(8,128)}) %all-gather.9.cloned.1.call-update) | async-done | bytes 1048592 | tf_op jit(solution)/shard_map/all_gather | solution.py:71
  1525.0 4.5 collective-permute-start.46
  1542.9 15.0 psum.122
  1557.9 62.5 %psum.123 = f32[128]{0:T(128)S(1)} all-reduce(f32[128]{0:T(128)S(1)} %psum.122), channel_id=1, replica_groups=mesh['sx'=8,'sy'=32] {'sy'}, use_global_device_ids=true, to_apply=%region_17.0 | all-reduce | flops 128 | bytes 1024 | tf_op jit(solution)/shard_map/psum | solution.py:98
  1622.8 4.6 multiply_reduce_fusion.1
  1627.4 74.3 %psum.124 = f32[128]{0:T(128)S(1)} all-reduce(f32[128]{0:T(128)S(1)} %get-tuple-element.42), channel_id=1, replica_groups=mesh['sx'=8,'sy'=32] {'sx','sy'}, use_global_device_ids=true, to_apply=%region_19.0 | all-reduce | flops 128 | bytes 1024 | tf_op jit(solution)/shard_map/psum | solution.py:78
  1731.6 263.0 %all-reduce.11.cloned.1.call-done = f32[2048,128]{1,0:T(8,128)} async-done(((f32[2048,128]{1,0:T(8,128)}), f32[2048,128]{1,0:T(8,128)}) %all-reduce.11.cloned.1.call-update) | async-done | bytes 1048592 | tf_op jit(solution)/shard_map/psum | solution.py:69
  1997.3 4.6 fusion.125
  2001.9 43.8 %all-gather.11.cloned.1.call-done = f32[2048,128]{1,0:T(8,128)} async-done(((f32[64,128]{1,0:T(8,128)}), f32[2048,128]{1,0:T(8,128)}) %all-gather.11.cloned.1.call-update) | async-done | bytes 1048592 | tf_op jit(solution)/shard_map/all_gather | solution.py:71
  2059.6 4.5 collective-permute-start.62
  2077.5 15.0 psum.126
  2092.5 62.5 %psum.127 = f32[128]{0:T(128)S(1)} all-reduce(f32[128]{0:T(128)S(1)} %psum.126), channel_id=1, replica_groups=mesh['sx'=8,'sy'=32] {'sy'}, use_global_device_ids=true, to_apply=%region_23.0 | all-reduce | flops 128 | bytes 1024 | tf_op jit(solution)/shard_map/psum | solution.py:98
  (290 shorter events, 248.3 us)
Async XLA Ops:
  7.2 302.0 %all-reduce.5.cloned.1.call-start = ((), (), s32[]{:S(2)}) async-start(), calls=%async_computation | async-start | bytes 2097152 | tf_op jit(solution)/shard_map/psum | solution.py:69
  11.3 15.6 collective-permute-start.5
  12.6 16.2 collective-permute-start.4
  17.6 14.8 collective-permute-start
  21.2 13.3 collective-permute-start.1
  43.7 316.9 %all-gather.5.cloned.1.call-start = ((), (), s32[]{:S(2)}) async-start(), calls=%async_computation.1 | async-start | bytes 1081344 | tf_op jit(solution)/shard_map/all_gather | solution.py:71
  311.8 613.8 %all-reduce.7.cloned.1.call-start = ((), (), s32[]{:S(2)}) async-start(), calls=%async_computation.2 | async-start | bytes 2097152 | tf_op jit(solution)/shard_map/psum | solution.py:69
  371.5 13.9 collective-permute-start.9
  373.4 16.7 collective-permute-start.14
  377.8 12.3 collective-permute-start.15
  633.8 13.4 collective-permute-start.21
  635.1 14.1 collective-permute-start.20
  639.5 13.4 collective-permute-start.16
  642.8 12.2 collective-permute-start.17
  664.1 312.8 %all-gather.7.cloned.1.call-start = ((), (), s32[]{:S(2)}) async-start(), calls=%async_computation.3 | async-start | bytes 1081344 | tf_op jit(solution)/shard_map/all_gather | solution.py:71
  928.2 531.9 %all-reduce.9.cloned.1.call-start = ((), (), s32[]{:S(2)}) async-start(), calls=%async_computation.4 | async-start | bytes 2097152 | tf_op jit(solution)/shard_map/psum | solution.py:69
  988.9 13.9 collective-permute-start.25
  990.8 16.7 collective-permute-start.30
  995.2 12.3 collective-permute-start.31
  1169.8 12.4 collective-permute-start.36
  1197.0 314.1 %all-gather.9.cloned.1.call-start = ((), (), s32[]{:S(2)}) async-start(), calls=%async_computation.5 | async-start | bytes 1081344 | tf_op jit(solution)/shard_map/all_gather | solution.py:71
  1462.7 531.9 %all-reduce.11.cloned.1.call-start = ((), (), s32[]{:S(2)}) async-start(), calls=%async_computation.6 | async-start | bytes 2097152 | tf_op jit(solution)/shard_map/psum | solution.py:69
  1523.1 13.9 collective-permute-start.41
  1525.0 16.7 collective-permute-start.46
  1529.5 12.3 collective-permute-start.47
  1704.3 12.4 collective-permute-start.52
  1708.4 12.0 collective-permute-start.48
  1710.3 12.0 collective-permute-start.49
  1731.6 314.1 %all-gather.11.cloned.1.call-start = ((), (), s32[]{:S(2)}) async-start(), calls=%async_computation.7 | async-start | bytes 1081344 | tf_op jit(solution)/shard_map/all_gather | solution.py:71
  2057.7 13.9 collective-permute-start.57
  2059.6 16.7 collective-permute-start.62
  2064.1 12.3 collective-permute-start.63
  (52 other events, 837.5 us)
Sparse Core Ops, SparseCore 0:
  43.8 265.3 all-reduce.4
  312.3 48.2 all-gather.4
  664.2 261.3 all-reduce.6
  928.6 48.2 all-gather.6
  1197.2 262.9 all-reduce.8
  1462.9 48.2 all-gather.8
  1731.7 262.8 all-reduce.10
  1997.4 48.2 all-gather.10
